TPU v7x, 1024 devices: a whole 4x4x32 slice. The times are simulated.
1024 devices in a mesh: feat: 128 (over x_hi, z, core), row: 4 (over y), rep: 2 (over x_lo).
Axes of the slice: x: 4 (x_hi: 2, x_lo: 2; x = x_hi * 2 + x_lo), y: 4, z: 32, core: 2. Of those that a mesh axis runs over, the one named last changes fastest.
Arguments:
- activations: bfloat16 [512, 4608], P('feat', ('row', 'rep')), may hold values from -6 to 6
- enc_weight: bfloat16 [4608, 65536], P(('row', 'rep'), 'feat'), may hold values from -0.09375 to 0.09375
- enc_bias: float32 [65536], P('feat'), may hold values from -3 to 3
- dec_weight: bfloat16 [65536, 4608], P('feat', ('row', 'rep')), may hold values from -0.0234375 to 0.0234375
- dec_bias: float32 [4608], P(('row', 'rep')), may hold values from -3 to 3
- first_moment: bfloat16 [65536, 4608], P('feat', ('row', 'rep')), may hold values from -0.059814453 to 0.059814453
- second_moment: bfloat16 [65536, 4608], P('feat', ('row', 'rep')), may hold values from 9.953976e-06 to 0.0009994507
Outputs:
- reconstruction: bfloat16 [512, 4608], P('feat', ('row', 'rep'))
- dec_step: bfloat16 [65536, 4608], P('feat', ('row', 'rep'))
All inputs are finite; a program needn't handle non-finite values.
Results may differ from a plain program's by a relative error of at most 0.0053.
Values may be sent and summed in bfloat16 or wider, within the bound.
A program may use at most 32 MiB of HBM per device.

v0:
```python
import jax
import jax.numpy as jnp
from jax import lax
from jax.sharding import PartitionSpec as P

sparsity_coef = 5.0
beta_one = 0.9
beta_two = 0.999
bias_one = 0.99997344
bias_two = 0.095207853
adam_eps = 1e-08
norm_eps = 1e-06


def shards(activations, enc_weight, enc_bias, dec_weight, dec_bias, first_moment, second_moment):
    local_rows = activations.shape[0]
    total_rows = local_rows * lax.axis_size("feat")
    centered = (activations.astype(jnp.float32) - dec_bias).astype(jnp.bfloat16)
    partial_value = jnp.dot(
        lax.all_gather(centered, "feat", axis=0, tiled=True),
        enc_weight,
        preferred_element_type=jnp.float32,
    )
    wide = dec_weight.astype(jnp.float32)
    squares = jnp.sum(wide * wide, axis=1)
    pre_sum, sum_squares = lax.psum((partial_value, squares), ("row", "rep"))
    active = jnp.maximum(pre_sum + enc_bias, 0.0).astype(jnp.bfloat16)
    rebuilt = (
        lax.psum_scatter(
            jnp.dot(active, dec_weight, preferred_element_type=jnp.float32),
            "feat",
            scatter_dimension=0,
            tiled=True,
        )
        + dec_bias
    )
    residual = (rebuilt - activations.astype(jnp.float32)).astype(jnp.bfloat16)
    all_residual = lax.all_gather(residual, "feat", axis=0, tiled=True)
    product = lax.dot_general(
        active, all_residual, (((0,), (0,)), ((), ())), preferred_element_type=jnp.float32
    )
    counts = jnp.sum(active.astype(jnp.float32), axis=0)
    row_norm = jnp.sqrt(sum_squares + norm_eps)
    gradient = (
        2.0 / total_rows * product
        + sparsity_coef / total_rows * counts[:, None] * wide / row_norm[:, None]
    )
    moment_one = beta_one * first_moment.astype(jnp.float32) + (1.0 - beta_one) * gradient
    moment_two = (
        beta_two * second_moment.astype(jnp.float32) + (1.0 - beta_two) * gradient * gradient
    )
    dec_step = (moment_one / bias_one / (jnp.sqrt(moment_two / bias_two) + adam_eps)).astype(
        jnp.bfloat16
    )
    return (rebuilt.astype(jnp.bfloat16), dec_step)


def solution(mesh):
    return jax.shard_map(
        shards,
        mesh=mesh,
        in_specs=(
            P("feat", ("row", "rep")),
            P(("row", "rep"), "feat"),
            P("feat"),
            P("feat", ("row", "rep")),
            P(("row", "rep")),
            P("feat", ("row", "rep")),
            P("feat", ("row", "rep")),
        ),
        out_specs=(P("feat", ("row", "rep")), P("feat", ("row", "rep"))),
        check_vma=False,
    )
```

profile of v0, /device:TPU:1, one launch (start us, length us, event | category | flops | bytes accessed | tf_op | source)
XLA Modules:
  0.0 1398.4 jit_solution(17029955297390839651)
XLA Ops:
  7.2 0.0 copy-start
  7.2 0.0 all-reduce.4.cloned.1.call-start
  7.2 0.8 fusion.13
  8.0 163.3 %all-gather = bf16[128,4,576]{2,1,0:T(4,128)(2,1)S(1)} all-gather(bf16[1,4,576]{2,1,0:T(4,128)(2,1)S(1)} %fusion.13), channel_id=1, replica_groups=mesh['feat'=128,'row'=4,'rep'=2] {'feat'}, dimensions={0}, use_global_device_ids=true | all-gather | bytes 594432 | tf_op jit(solution)/shard_map/all_gather | solution.py:20
  171.3 0.3 reshape.12
  171.6 0.0 copy-done
  171.6 0.0 copy-start.4
  171.7 1.6 fusion.14
  173.3 0.0 copy-start.1
  173.3 0.0 all-reduce.4.cloned.1.call-update
  173.3 0.0 all-reduce.6.cloned.1.call-start
  173.3 90.9 %all-reduce.4.cloned.1.call-done = f32[512,512]{1,0:T(8,128)} async-done(((f32[512,512]{1,0:T(8,128)}), f32[512,512]{1,0:T(8,128)}) %all-reduce.4.cloned.1.call-update) | async-done | bytes 1048592 | tf_op jit(solution)/shard_map/psum | solution.py:26
  264.3 0.0 copy-done.4
  264.3 1.4 convert_reduce_fusion
  265.7 0.0 copy-done.1
  265.7 1.7 fusion.15
  267.4 0.0 copy-start.2
  267.4 0.0 copy-start.3
  267.4 0.0 all-reduce.6.cloned.1.call-update
  267.4 1.3 dynamic-slice
  269.4 0.2 fusion.2
  269.5 15.2 %psum.15 = f32[512]{0:T(512)S(1)} all-reduce(f32[512]{0:T(512)S(1)} %fusion.2), channel_id=1, replica_groups=mesh['feat'=128,'row'=4,'rep'=2] {'row','rep'}, use_global_device_ids=true, to_apply=%region_4.0 | all-reduce | flops 512 | bytes 4096 | tf_op jit(solution)/shard_map/psum | solution.py:26
  284.7 958.0 %all-reduce.6.cloned.1.call-done = f32[512,576]{1,0:T(8,128)} async-done(((f32[512,576]{1,0:T(8,128)}), f32[512,576]{1,0:T(8,128)}) %all-reduce.6.cloned.1.call-update) | async-done | bytes 1179664
  1242.7 0.0 copy-done.2
  1242.7 0.0 copy-done.3
  1242.7 1.3 fusion.12
  1244.0 143.8 %all-gather.1 = bf16[128,4,576]{2,1,0:T(4,128)(2,1)S(1)} all-gather(bf16[1,4,576]{2,1,0:T(4,128)(2,1)S(1)} %get-tuple-element.4), channel_id=1, replica_groups=mesh['feat'=128,'row'=4,'rep'=2] {'feat'}, dimensions={0}, use_global_device_ids=true | all-gather | bytes 594432 | tf_op jit(solution)/shard_map/all_gather | solution.py:38
  1387.8 0.3 reshape.14
  1388.1 3.5 fusion.8
  (2 shorter events, 0.0 us)
Async XLA Ops:
  7.2 164.5 %copy-start = (bf16[576,512]{1,0:T(8,128)(2,1)S(1)}, bf16[576,512]{1,0:T(8,128)(2,1)}, u32[]{:S(2)}) copy-start(bf16[576,512]{1,0:T(8,128)(2,1)} %param.8) | copy-start | bytes 1769476
  7.2 257.1 %all-reduce.4.cloned.1.call-start = ((), (), s32[]{:S(2)}) async-start(), calls=%async_computation | async-start | bytes 2097152 | tf_op jit(solution)/shard_map/psum | solution.py:26
  171.6 92.6 %copy-start.4 = (f32[512]{0:T(512)S(1)}, f32[512]{0:T(512)}, u32[]{:S(2)}) copy-start(f32[512]{0:T(512)} %param.9) | copy-start | bytes 6148
  173.3 92.4 %copy-start.1 = (bf16[512,576]{0,1:T(8,128)(2,1)S(1)}, bf16[512,576]{0,1:T(8,128)(2,1)}, u32[]{:S(2)}) copy-start(bf16[512,576]{0,1:T(8,128)(2,1)} %param.10) | copy-start | bytes 1769476
  173.3 1069.4 %all-reduce.6.cloned.1.call-start = ((), (), s32[]{:S(2)}) async-start(), calls=%async_computation.1 | async-start | bytes 2621440
  267.4 975.3 %copy-start.2 = (bf16[4,576]{1,0:T(4,128)(2,1)S(1)}, bf16[4,576]{1,0:T(4,128)(2,1)}, u32[]{:S(2)}) copy-start(bf16[4,576]{1,0:T(4,128)(2,1)} %param.7) | copy-start | bytes 13828
  267.4 975.3 %copy-start.3 = (f32[576]{0:T(1024)S(1)}, f32[576]{0:T(1024)}, u32[]{:S(2)}) copy-start(f32[576]{0:T(1024)} %param.11) | copy-start | bytes 6916
Sparse Core Ops, SparseCore 0:
  173.4 90.8 all-reduce.3
  267.8 974.8 all-reduce.5
where the time goes:
time: 1400 us
  waiting for transfers between devices  1050 us (75%)
  blocking collectives  322 us (23%)
  between operations  14.7 us (1%)
    unnamed x3, waiting for transfers between devices  958 us
    all_gather x1, blocking collectives, shards(): lax.all_gather(centered, 'feat', axis=0, tiled=True)  163 us
    all_gather x1, blocking collectives, shards(): all_residual = lax.all_gather(residual, 'feat', axis=0, tiled=True)  144 us
    psum x1, waiting for transfers between devices, shards(): pre_sum, sum_squares = lax.psum((partial_value, squares), ('row', 'rep'))  90.9 us
  transfers between devices with their start and end apart: 2, of which 2 were waited for; matrix products, arithmetic and copies ran while one was open for 0% of the time, Pallas kernels for 0%

commit v1 on v0

v1 whole, which is shorter than its diff:
```python
import jax
import jax.numpy as jnp
from jax import lax
from jax.experimental import pallas as pl
from jax.experimental.pallas import tpu as pltpu
from jax.sharding import PartitionSpec as P

sparsity_coef = 5.0
beta_one = 0.9
beta_two = 0.999
bias_one = 0.99997344
bias_two = 0.095207853
adam_eps = 1e-08
norm_eps = 1e-06

MESH = pl.DeviceIdType.MESH
F32 = jnp.float32
BF16 = jnp.bfloat16


def make_kernel(nz, rows, reps, local_rows, width, feats):
    half = nz // 2
    peers = rows * reps
    chip_rows = 2 * local_rows
    total_rows = 2 * nz * chip_rows
    group = total_rows // peers
    per_far = peers // 2
    blocks = group // chip_rows
    core_groups = per_far // 2

    def kernel(
        act_ref, enc_hbm, ebias_ref, dec_hbm, dbias_ref, first_hbm, second_hbm,
        recon_ref, step_hbm,
        enc, dec, first, second, step, load_sem, store_sem,
        act_send, act_recv, acts, gathered, block, partial, sums_out, sums_in, active, active_t,
        squares_out, squares_in, product, core_in, x_out, x_in, z_out, z_in, total_out, total_in, residuals, coef,
        pair_send, pair_recv, z_send, z_recv, zr_send, zr_recv, za_send, za_recv,
        peer_send, peer_recv, sq_send, sq_recv, ac_send, ac_recv,
    ):
        feat = lax.axis_index("feat")
        row, rep = lax.axis_index("row"), lax.axis_index("rep")
        far_x = lax.div(feat, 2 * nz)
        z = lax.rem(lax.div(feat, 2), nz)
        core = lax.rem(feat, 2)
        k = row * reps + rep

        def at_z(where):
            return (far_x * (2 * nz) + lax.rem(where + 2 * nz, nz) * 2 + core, row, rep)

        other_core = (feat + 1 - 2 * core, row, rep)
        other_x = (lax.rem(feat + 2 * nz, 4 * nz), row, rep)

        def peer(j):
            p = lax.rem(k + j, peers)
            return (feat, lax.div(p, reps), lax.rem(p, reps))

        loads = [
            pltpu.make_async_copy(src, dst, load_sem.at[i])
            for i, (src, dst) in enumerate(
                ((dec_hbm, dec), (enc_hbm, enc), (first_hbm, first), (second_hbm, second))
            )
        ]
        for load in loads:
            load.start()

        barrier = pltpu.get_barrier_semaphore()

        def greet(device):
            pl.semaphore_signal(barrier, inc=1, device_id=device, device_id_type=MESH)

        low = core * half

        @pl.loop(0, half)
        def _(i):
            s = low + i

            @pl.when(s > 0)
            def _():
                greet(at_z(z + s))
                greet(at_z(z - s))

        greet(other_core)
        greet(other_x)

        @pl.loop(1, peers)
        def _(j):
            greet(peer(j))

        act_send[...] = act_ref[...]
        loads[0].wait()
        wide = dec[...].astype(F32)
        square = wide * wide
        high = square.astype(BF16)
        rest = (square - high.astype(F32)).astype(BF16)
        ones = jnp.ones((8, width), BF16)
        along = (((1,), (1,)), ((), ()))
        squares_out[...] = lax.dot_general(ones, high, along, preferred_element_type=F32) + lax.dot_general(
            ones, rest, along, preferred_element_type=F32
        )
        pl.semaphore_wait(barrier, 2 * half - 2 * (1 - core) + 2 + peers - 1)

        def pair(src, dst, i, device):
            return pltpu.make_async_remote_copy(
                src_ref=src, dst_ref=dst, send_sem=pair_send.at[i], recv_sem=pair_recv.at[i],
                device_id=device, device_id_type=MESH,
            )

        def square_copy(j):
            return pltpu.make_async_remote_copy(
                src_ref=squares_out, dst_ref=squares_in.at[j], send_sem=sq_send.at[j], recv_sem=sq_recv.at[j],
                device_id=peer(j), device_id_type=MESH,
            )

        swap = pair(act_send, act_recv, 0, other_core)
        swap.start()
        swap.wait()
        own, his = act_send[...].astype(F32), act_recv[...].astype(F32)
        acts[0:local_rows] = jnp.where(core == 0, own, his)
        acts[local_rows:] = jnp.where(core == 0, his, own)
        block[...] = (acts[...] - dbias_ref[...]).astype(BF16)

        def gather(src, buffer, send, recv, first_pair, between):
            def z_copy(i):
                s = jnp.where(core == 0, half - 1 - i, half + i)
                return s, pltpu.make_async_remote_copy(
                    src_ref=src, dst_ref=buffer.at[0, s], send_sem=send.at[i], recv_sem=recv.at[i],
                    device_id=at_z(z + s), device_id_type=MESH,
                )

            @pl.loop(0, half)
            def _(i):
                s, copy = z_copy(i)

                @pl.when(s > 0)
                def _():
                    copy.start()

            @pl.when(core == 0)
            def _():
                buffer[0, 0] = src[...]

            between()

            @pl.loop(0, half)
            def _(i):
                s, copy = z_copy(i)

                @pl.when(s > 0)
                def _():
                    copy.wait_recv()

            mine = pl.ds(low, half)
            to_x = pair(buffer.at[0, mine], buffer.at[1, mine], first_pair, other_x)
            to_core = pair(buffer.at[0, mine], buffer.at[0, mine], first_pair + 1, other_core)
            on_core = pair(buffer.at[1, mine], buffer.at[1, mine], first_pair + 2, other_core)
            to_x.start()
            to_core.start()
            return to_x, to_core, on_core, z_copy

        def finish_sends(z_copy):
            @pl.loop(0, half)
            def _(i):
                s, copy = z_copy(i)

                @pl.when(s > 0)
                def _():
                    copy.wait_send()

        def during_first():
            @pl.loop(1, peers)
            def _(j):
                square_copy(j).start()

            loads[1].wait()

        to_x, to_core, on_core, z_copy_a = gather(block, gathered, z_send, z_recv, 1, during_first)

        def sum_copy(j):
            p = lax.rem(k + j, peers)
            return p, pltpu.make_async_remote_copy(
                src_ref=sums_out.at[p], dst_ref=sums_in.at[j], send_sem=peer_send.at[j], recv_sem=peer_recv.at[j],
                device_id=peer(j), device_id_type=MESH,
            )

        def encode(far):
            rows_in = gathered[far].reshape(nz * chip_rows, width)
            value = jnp.dot(rows_in, enc[...], preferred_element_type=F32).reshape(per_far, group, feats)
            partial[far * per_far : (far + 1) * per_far] = value
            sums_out[far * per_far : (far + 1) * per_far] = value.astype(BF16)

            @pl.loop(1, peers)
            def _(j):
                p, copy = sum_copy(j)

                @pl.when(lax.div(p, per_far) == far)
                def _():
                    copy.start()

        to_core.wait_recv()
        encode(0)
        to_x.wait_recv()
        on_core.start()
        on_core.wait_recv()
        encode(1)

        pre_sum = partial[k] + ebias_ref[...]
        for j in range(1, peers):
            sum_copy(j)[1].wait_recv()
            pre_sum += sums_in[j].astype(F32)
        active[k] = jnp.maximum(pre_sum, 0.0).astype(BF16)

        def active_copy(j):
            return pltpu.make_async_remote_copy(
                src_ref=active.at[k], dst_ref=active.at[k], send_sem=ac_send.at[j], recv_sem=ac_recv.at[j],
                device_id=peer(j), device_id_type=MESH,
            )

        @pl.loop(1, peers)
        def _(j):
            active_copy(j).start()

        @pl.loop(1, peers)
        def _(j):
            active_copy(j).wait_recv()

        his_low = half - low

        def decode(far, who):
            rows_in = active[pl.ds(far * per_far + who * core_groups, core_groups)]
            value = jnp.dot(
                rows_in.reshape(half * chip_rows, feats), dec[...], preferred_element_type=F32
            )
            product[far, pl.ds(who * half, half)] = value.reshape(half, chip_rows, width)

        core_copies = [
            pair(product.at[far, pl.ds(his_low, half)], core_in.at[far], 4 + far, other_core) for far in (0, 1)
        ]
        decode(1, 1 - core)
        core_copies[1].start()
        decode(0, 1 - core)
        core_copies[0].start()
        decode(1, core)
        core_copies[1].wait_recv()
        x_out[...] = (product[1, pl.ds(low, half)] + core_in[1]).astype(BF16)
        over = pair(x_out, x_in, 6, other_x)
        over.start()
        decode(0, core)
        core_copies[0].wait_recv()
        near = product[0, pl.ds(low, half)] + core_in[0]
        over.wait_recv()
        z_out[...] = (near + x_in[...].astype(F32)).astype(BF16)

        def back_copy(i):
            place = jnp.where(core == 0, half - 1 - i, i)
            s = low + place
            return s, pltpu.make_async_remote_copy(
                src_ref=z_out.at[place], dst_ref=z_in.at[place], send_sem=zr_send.at[i], recv_sem=zr_recv.at[i],
                device_id=at_z(z - s), device_id_type=MESH,
            )

        @pl.loop(0, half)
        def _(i):
            s, copy = back_copy(i)

            @pl.when(s > 0)
            def _():
                copy.start()

        @pl.when(core == 0)
        def _():
            z_in[0] = z_out[0]

        flat = active[...].reshape(total_rows, feats)
        active_t[...] = flat.T
        counts = jnp.dot(active_t[...], jnp.ones((total_rows, 128), BF16), preferred_element_type=F32)
        sum_squares = squares_out[...]
        for j in range(1, peers):
            square_copy(j).wait_recv()
            sum_squares += squares_in[j]
        norm = jnp.sqrt(sum_squares[0:1] + norm_eps)
        norm = jnp.broadcast_to(norm, (128, feats)).T
        coef[...] = sparsity_coef / total_rows * counts / norm

        @pl.loop(0, half)
        def _(i):
            s, copy = back_copy(i)

            @pl.when(s > 0)
            def _():
                copy.wait_recv()

        total_out[...] = jnp.sum(z_in[...].astype(F32), axis=0)
        both = pair(total_out, total_in, 7, other_core)
        both.start()
        both.wait_recv()
        rebuilt = total_out[...] + total_in[...] + dbias_ref[...]
        recon_ref[...] = jnp.where(core == 0, rebuilt[0:local_rows], rebuilt[local_rows:]).astype(BF16)
        block_two = z_out.at[0]
        finish_sends(back_copy)
        block_two[...] = (rebuilt - acts[...]).astype(BF16)

        def during_last():
            loads[2].wait()
            loads[3].wait()

        to_x_two, to_core_two, on_core_two, z_copy_b = gather(
            block_two, residuals, za_send, za_recv, 8, during_last
        )
        to_core_two.wait_recv()
        to_x_two.wait_recv()
        on_core_two.start()
        on_core_two.wait_recv()
        all_residual = residuals[...].reshape(total_rows, width)

        part = feats // 4

        def store(i):
            where = pl.ds(i * part, part)
            return pltpu.make_async_copy(step.at[where], step_hbm.at[where], store_sem.at[i])

        for i in range(4):
            where = slice(i * part, (i + 1) * part)
            gradient = 2.0 / total_rows * jnp.dot(
                active_t[where], all_residual, preferred_element_type=F32
            ) + coef[where, 0:1] * dec[where].astype(F32)
            moment_one = beta_one * first[where].astype(F32) + (1.0 - beta_one) * gradient
            moment_two = beta_two * second[where].astype(F32) + (1.0 - beta_two) * gradient * gradient
            step[where] = (
                moment_one * (1.0 / bias_one) / (jnp.sqrt(moment_two * (1.0 / bias_two)) + adam_eps)
            ).astype(BF16)
            store(i).start()

        finish_sends(z_copy_a)
        finish_sends(z_copy_b)
        for copy in (to_x, to_core, on_core, *core_copies, over, both, to_x_two, to_core_two, on_core_two):
            copy.wait_send()

        @pl.loop(1, peers)
        def _(j):
            square_copy(j).wait_send()
            sum_copy(j)[1].wait_send()
            active_copy(j).wait_send()

        for i in range(4):
            store(i).wait()

    scratch = [
        pltpu.VMEM((width, feats), BF16),
        pltpu.VMEM((feats, width), BF16),
        pltpu.VMEM((feats, width), BF16),
        pltpu.VMEM((feats, width), BF16),
        pltpu.VMEM((feats, width), BF16),
        pltpu.SemaphoreType.DMA((4,)),
        pltpu.SemaphoreType.DMA((4,)),
        pltpu.VMEM((local_rows, width), BF16),
        pltpu.VMEM((local_rows, width), BF16),
        pltpu.VMEM((chip_rows, width), F32),
        pltpu.VMEM((2, nz, chip_rows, width), BF16),
        pltpu.VMEM((chip_rows, width), BF16),
        pltpu.VMEM((peers, group, feats), F32),
        pltpu.VMEM((peers, group, feats), BF16),
        pltpu.VMEM((peers, group, feats), BF16),
        pltpu.VMEM((peers, group, feats), BF16),
        pltpu.VMEM((feats, total_rows), BF16),
        pltpu.VMEM((8, feats), F32),
        pltpu.VMEM((peers, 8, feats), F32),
        pltpu.VMEM((2, nz, chip_rows, width), F32),
        pltpu.VMEM((2, half, chip_rows, width), F32),
        pltpu.VMEM((half, chip_rows, width), BF16),
        pltpu.VMEM((half, chip_rows, width), BF16),
        pltpu.VMEM((half, chip_rows, width), BF16),
        pltpu.VMEM((half, chip_rows, width), BF16),
        pltpu.VMEM((chip_rows, width), F32),
        pltpu.VMEM((chip_rows, width), F32),
        pltpu.VMEM((2, nz, chip_rows, width), BF16),
        pltpu.VMEM((feats, 128), F32),
        pltpu.SemaphoreType.DMA((11,)),
        pltpu.SemaphoreType.DMA((11,)),
        *(pltpu.SemaphoreType.DMA((half,)) for _ in range(6)),
        *(pltpu.SemaphoreType.DMA((peers,)) for _ in range(6)),
    ]
    return kernel, scratch


def shards(nz, rows, reps, activations, enc_weight, enc_bias, dec_weight, dec_bias, first_moment, second_moment):
    local_rows, width = activations.shape
    feats = enc_weight.shape[1]
    kernel, scratch = make_kernel(nz, rows, reps, local_rows, width, feats)
    vmem = pl.BlockSpec(memory_space=pltpu.VMEM)
    hbm = pl.BlockSpec(memory_space=pl.ANY)
    return pl.pallas_call(
        kernel,
        out_shape=(
            jax.ShapeDtypeStruct((local_rows, width), BF16),
            jax.ShapeDtypeStruct((feats, width), BF16),
        ),
        in_specs=[vmem, hbm, vmem, hbm, vmem, hbm, hbm],
        out_specs=(vmem, hbm),
        scratch_shapes=scratch,
        compiler_params=pltpu.CompilerParams(
            collective_id=0, has_side_effects=True, vmem_limit_bytes=48 * 2**20
        ),
    )(activations, enc_weight, enc_bias[None, :], dec_weight, dec_bias[None, :], first_moment, second_moment)


def solution(mesh):
    nz, rows, reps = mesh.shape["feat"] // 4, mesh.shape["row"], mesh.shape["rep"]

    def step(*args):
        return shards(nz, rows, reps, *args)

    return jax.shard_map(
        step,
        mesh=mesh,
        in_specs=(
            P("feat", ("row", "rep")),
            P(("row", "rep"), "feat"),
            P("feat"),
            P("feat", ("row", "rep")),
            P(("row", "rep")),
            P("feat", ("row", "rep")),
            P("feat", ("row", "rep")),
        ),
        out_specs=(P("feat", ("row", "rep")), P("feat", ("row", "rep"))),
        check_vma=False,
    )
```

time: 1400 us -> 140 us (0.10)
  waiting for transfers between devices: 1050 us -> 0 us
  blocking collectives: 322 us -> 0 us
  Pallas kernels: 0 us -> 133 us
  between operations: 14.7 us -> 0.67 us
    unnamed x3 -> x0, waiting for transfers between devices: 958 us -> none
    all_gather x2 -> x0, blocking collectives: 307 us -> none  [the longest x1 163 us: shards(): lax.all_gather(centered, 'feat', axis=0, tiled=True)]
    pallas_call x0 -> x1, Pallas kernels: none -> 133 us  [shards(): pl.pallas_call(kernel, out_shape=(jax.ShapeDtypeStruct((local_rows, width...]
    psum x1 -> x0, waiting for transfers between devices: 90.9 us -> none  [shards(): pre_sum, sum_squares = lax.psum((partial_value, squares), ('row', 'rep'))]
    psum x1 -> x0, blocking collectives: 15.2 us -> none  [shards(): pre_sum, sum_squares = lax.psum((partial_value, squares), ('row', 'rep'))]
  transfers between devices with their start and end apart: 2 -> 0, of which waited for: 2 -> 0; matrix products, arithmetic and copies ran while one was open for 0% -> 0% of each run, Pallas kernels for 0% -> 0%
where the time goes in v1:
time: 140 us
  Pallas kernels  133 us (95%)
  local copies, waits for them, and re-layouts  5.88 us (4%)
    pallas_call x1, Pallas kernels, shards(): pl.pallas_call(kernel, out_shape=(jax.ShapeDtypeStruct((local_rows, width...  133 us
    unnamed x14, local copies, waits for them, and re-layouts  4.13 us

profile of v1, /device:TPU:1, one launch (start us, length us, event | category | flops | bytes accessed | tf_op | source)
XLA Modules:
  0.0 140.0 jit_solution(11834079612700373237)
XLA Ops:
  0.6 0.7 broadcast_in_dim.7.dbias_ref
  1.3 0.0 copy-start.3
  1.3 1.4 %copy.9.dec_hbm = bf16[512,576]{1,0:T(8,128)(2,1)S(1)} copy(bf16[512,576]{0,1:T(8,128)(2,1)} %param.10) | data formatting | bytes 1179648 | tf_op args[3]
  2.7 0.0 copy-done.3
  2.8 0.0 copy-start.4
  2.8 0.3 copy.10.first_hbm
  3.1 0.8 copy-done.4
  3.8 0.0 copy-start
  3.8 0.0 copy-start.1
  3.8 0.0 copy-start.2
  3.8 0.3 copy.11.second_hbm
  4.1 0.8 copy-done
  4.9 0.0 copy-done.1
  4.9 0.0 copy-done.2
  4.9 133.5 %shard_map.86 = (bf16[4,576]{1,0:T(4,128)(2,1)S(1)}, bf16[512,576]{1,0:T(8,128)(2,1)S(1)}) custom-call(bf16[4,576]{1,0:T(4,128)(2,1)S(1)} %copy-done.1, bf16[576,512]{1,0:T(8,128)(2,1)S(1)} %copy-done, f32[1,512]{1,0:T(1,128)S(1)} %bitcast.1, bf16[512,576]{1,0:T(8,128)(2,1)S(1)} %copy.9.dec_hbm, f32[1,576]{1,0:T(1,128)S(1)} %broadcast_in_dim.7.dbias_ref, ...), custom_call_target="tpu_custom_call" | custom-call | tf_op jit(solution)/shard_map/pallas_call | solution.py:391
  138.4 1.1 copy.12
  139.5 0.6 copy.14
Async XLA Ops:
  1.3 1.4 %copy-start.3 = (bf16[512,576]{0,1:T(8,128)(2,1)S(1)}, bf16[512,576]{0,1:T(8,128)(2,1)}, u32[]{:S(2)}) copy-start(bf16[512,576]{0,1:T(8,128)(2,1)} %param.12) | copy-start | bytes 1769476
  2.8 1.1 copy-start.4
  3.8 1.1 copy-start
  3.8 1.1 copy-start.1
  3.8 1.1 copy-start.2

commit v2 on v1

v2 whole, which is shorter than its diff:
```python
import jax
import jax.numpy as jnp
from jax import lax
from jax.experimental import pallas as pl
from jax.experimental.pallas import tpu as pltpu
from jax.sharding import PartitionSpec as P

sparsity_coef = 5.0
beta_one = 0.9
beta_two = 0.999
bias_one = 0.99997344
bias_two = 0.095207853
adam_eps = 1e-08
norm_eps = 1e-06

MESH = pl.DeviceIdType.MESH
F32 = jnp.float32
BF16 = jnp.bfloat16


def make_kernel(nz, rows, reps, local_rows, width, feats):
    near = (0, 1, 2, -1)
    window = len(near)
    per_chip = nz // window
    per_core = per_chip // 2
    chip_rows = 2 * local_rows
    total_rows = 2 * nz * chip_rows
    half_rows = total_rows // 2
    peers = rows * reps
    group = total_rows // peers
    core_rows = per_core * chip_rows
    assert peers == 2 * window and group == 2 * core_rows
    around = [(far, w) for far in (1, 0) for w in range(window) if (far, w) != (0, 0)]

    def kernel(
        act_ref, enc_hbm, ebias_ref, dec_hbm, dbias_ref, first_hbm, second_hbm,
        recon_ref, step_hbm,
        enc, dec, first, second, step, load_sem, store_sem,
        act_send, act_recv, acts, gathered, block, partial, sums_out, sums_in, active,
        squares_out, squares_in, product, core_in, parts_out, parts_in, z_out, z_in, total_out, total_in, residuals,
        block_two, coef, residual_t, slope,
        pair_send, pair_recv, z_send, z_recv, zr_send, zr_recv, za_send, za_recv,
        x_send, x_recv, c_send, c_recv, part_send, part_recv, xa_send, xa_recv, ca_send, ca_recv,
        peer_send, peer_recv, sq_send, sq_recv, ac_send, ac_recv,
    ):
        feat = lax.axis_index("feat")
        row, rep = lax.axis_index("row"), lax.axis_index("rep")
        far_x = lax.div(feat, 2 * nz)
        z = lax.rem(lax.div(feat, 2), nz)
        core = lax.rem(feat, 2)
        k = row * reps + rep

        def chip(far, where):
            x = lax.rem(far_x + far, 2)
            return (x * (2 * nz) + lax.rem(where + 2 * nz, nz) * 2 + core, row, rep)

        other_core = (feat + 1 - 2 * core, row, rep)

        def peer(j):
            p = lax.rem(k + j, peers)
            return (feat, lax.div(p, reps), lax.rem(p, reps))

        loads = [
            pltpu.make_async_copy(src, dst, load_sem.at[i])
            for i, (src, dst) in enumerate(
                ((dec_hbm, dec), (enc_hbm, enc), (first_hbm, first), (second_hbm, second))
            )
        ]
        for load in loads:
            load.start()

        barrier = pltpu.get_barrier_semaphore()

        def greet(device):
            pl.semaphore_signal(barrier, inc=1, device_id=device, device_id_type=MESH)

        def far_first(j):
            m = jnp.where(core == 0, j, per_chip - 1 - j)
            return m, m != per_core

        @pl.loop(0, per_core)
        def _(j):
            m, remote = far_first(j)

            @pl.when(remote)
            def _():
                greet(chip(0, z + window * (per_core - m)))
                greet(chip(0, z - window * (per_core - m)))

        beside = sorted({(far, side * near[w]) for far, w in around for side in (1, -1)})
        for far, offset in beside:
            greet(chip(far, z + offset))
        greet(other_core)

        @pl.loop(1, peers)
        def _(j):
            greet(peer(j))

        act_send[...] = act_ref[...]
        loads[0].wait()
        wide = dec[...].astype(F32)
        square = wide * wide
        high = square.astype(BF16)
        rest = (square - high.astype(F32)).astype(BF16)
        ones = jnp.ones((8, width), BF16)
        squares_out[...] = jnp.dot(ones, high, preferred_element_type=F32) + jnp.dot(
            ones, rest, preferred_element_type=F32
        )
        pl.semaphore_wait(barrier, 2 * per_core - 2 * core + len(beside) + peers)

        def pair(src, dst, i, device):
            return pltpu.make_async_remote_copy(
                src_ref=src, dst_ref=dst, send_sem=pair_send.at[i], recv_sem=pair_recv.at[i],
                device_id=device, device_id_type=MESH,
            )

        def square_copy(j):
            return pltpu.make_async_remote_copy(
                src_ref=squares_out, dst_ref=squares_in.at[j], send_sem=sq_send.at[j], recv_sem=sq_recv.at[j],
                device_id=peer(j), device_id_type=MESH,
            )

        swap = pair(act_send, act_recv, 0, other_core)
        swap.start()
        swap.wait()
        own, his = act_send[...].astype(F32), act_recv[...].astype(F32)
        acts[0:local_rows] = jnp.where(core == 0, own, his)
        acts[local_rows:] = jnp.where(core == 0, his, own)
        block[...] = (acts[...] - dbias_ref[...].reshape(1, width)).astype(BF16)

        def each_far(action):
            @pl.loop(0, per_core)
            def _(j):
                m, remote = far_first(j)

                @pl.when(remote)
                def _():
                    action(m)

        mine = pl.ds(core * per_core, per_core)

        def gather(src, buffer, z_sems, x_sems, core_sems, between):
            def z_copy(m):
                return pltpu.make_async_remote_copy(
                    src_ref=src, dst_ref=buffer.at[0, 0, m], send_sem=z_sems[0].at[m], recv_sem=z_sems[1].at[m],
                    device_id=chip(0, z + window * (per_core - m)), device_id_type=MESH,
                )

            def beside_copy(far, w):
                return pltpu.make_async_remote_copy(
                    src_ref=buffer.at[0, 0, mine], dst_ref=buffer.at[far, w, mine],
                    send_sem=x_sems[0].at[far * window + w], recv_sem=x_sems[1].at[far * window + w],
                    device_id=chip(far, z + near[w]), device_id_type=MESH,
                )

            def core_copy(far, w):
                return pltpu.make_async_remote_copy(
                    src_ref=buffer.at[far, w, mine], dst_ref=buffer.at[far, w, mine],
                    send_sem=core_sems[0].at[far * window + w], recv_sem=core_sems[1].at[far * window + w],
                    device_id=other_core, device_id_type=MESH,
                )

            each_far(lambda m: z_copy(m).start())

            @pl.when(core == 1)
            def _():
                buffer[0, 0, per_core] = src[...]

            between()
            each_far(lambda m: z_copy(m).wait_recv())
            for far, w in around:
                beside_copy(far, w).start()
            core_copy(0, 0).start()

            def arrive(far):
                for w in range(window):
                    if (far, w) != (0, 0):
                        beside_copy(far, w).wait_recv()
                        core_copy(far, w).start()
                for w in range(window):
                    core_copy(far, w).wait_recv()

            def finish():
                each_far(lambda m: z_copy(m).wait_send())
                for far, w in around:
                    beside_copy(far, w).wait_send()
                    core_copy(far, w).wait_send()
                core_copy(0, 0).wait_send()

            return arrive, finish

        def during_first():
            @pl.loop(1, peers)
            def _(j):
                square_copy(j).start()

            loads[1].wait()

        arrive, finish_first = gather(
            block, gathered, (z_send, z_recv), (x_send, x_recv), (c_send, c_recv), during_first
        )

        def sum_copy(j):
            p = lax.rem(k + j, peers)
            return p, pltpu.make_async_remote_copy(
                src_ref=sums_out.at[p], dst_ref=sums_in.at[j], send_sem=peer_send.at[j], recv_sem=peer_recv.at[j],
                device_id=peer(j), device_id_type=MESH,
            )

        def encode(far):
            rows_in = gathered[far].reshape(half_rows, width)
            value = jnp.dot(rows_in, enc[...], preferred_element_type=F32).reshape(window, group, feats)
            partial[far * window : (far + 1) * window] = value
            sums_out[far * window : (far + 1) * window] = value.astype(BF16)

            @pl.loop(1, peers)
            def _(j):
                p, copy = sum_copy(j)

                @pl.when(lax.div(p, window) == far)
                def _():
                    copy.start()

        arrive(0)
        encode(0)
        arrive(1)
        encode(1)

        pre_sum = partial[k] + ebias_ref[...].reshape(1, feats)
        for j in range(1, peers):
            sum_copy(j)[1].wait_recv()
            pre_sum += sums_in[j].astype(F32)
        active[k] = jnp.maximum(pre_sum, 0.0).reshape(2, core_rows, feats).astype(BF16)

        def active_copy(j):
            return pltpu.make_async_remote_copy(
                src_ref=active.at[k], dst_ref=active.at[k], send_sem=ac_send.at[j], recv_sem=ac_recv.at[j],
                device_id=peer(j), device_id_type=MESH,
            )

        @pl.loop(1, peers)
        def _(j):
            active_copy(j).start()

        def wait_active(far):
            @pl.loop(1, peers)
            def _(j):
                @pl.when(lax.div(lax.rem(k - j + peers, peers), window) == far)
                def _():
                    active_copy(j).wait_recv()

        def decode(far, who):
            value = lax.dot_general(
                active[far * window : (far + 1) * window, who].reshape(window * core_rows, feats),
                dec[...], (((1,), (1,)), ((), ())), preferred_element_type=F32,
            )
            product[far, who] = value.reshape(window, core_rows, width)

        core_parts = [pair(product.at[far, 1 - core], core_in.at[far], 1 + far, other_core) for far in (0, 1)]

        def part_copy(far, w):
            return pltpu.make_async_remote_copy(
                src_ref=parts_out.at[far, w], dst_ref=parts_in.at[far * window + w],
                send_sem=part_send.at[far * window + w], recv_sem=part_recv.at[far * window + w],
                device_id=chip(far, z - near[w]), device_id_type=MESH,
            )

        def hand_out(far):
            core_parts[far].wait_recv()
            both_cores = product[far, core] + core_in[far]
            parts_out[far] = both_cores.astype(BF16)
            for other, w in around:
                if other == far:
                    part_copy(far, w).start()
            return both_cores

        wait_active(0)
        decode(0, 1 - core)
        core_parts[0].start()
        decode(0, core)
        wait_active(1)
        decode(1, 1 - core)
        core_parts[1].start()
        own_part = hand_out(0)[0]
        decode(1, core)
        hand_out(1)
        for far, w in reversed(around):
            part_copy(far, w).wait_recv()
            own_part += parts_in[far * window + w].astype(F32)
        z_out[...] = own_part.reshape(per_core, chip_rows, width).astype(BF16)

        def back_copy(m):
            place = m - core * per_core
            return pltpu.make_async_remote_copy(
                src_ref=z_out.at[place], dst_ref=z_in.at[place], send_sem=zr_send.at[m], recv_sem=zr_recv.at[m],
                device_id=chip(0, z + window * (m - per_core)), device_id_type=MESH,
            )

        each_far(lambda m: back_copy(m).start())

        @pl.when(core == 1)
        def _():
            z_in[0] = z_out[0]

        flat = active[...].reshape(total_rows, feats)
        counts = jnp.dot(jnp.ones((8, total_rows), BF16), flat, preferred_element_type=F32)
        sum_squares = squares_out[...]
        for j in range(1, peers):
            square_copy(j).wait_recv()
            sum_squares += squares_in[j]
        norm = jnp.sqrt(sum_squares[0:1] + norm_eps)
        coef[...] = sparsity_coef / total_rows * counts[0:1] / norm

        each_far(lambda m: back_copy(m).wait_recv())
        total_out[...] = jnp.sum(z_in[...].astype(F32), axis=0)
        both = pair(total_out, total_in, 3, other_core)
        both.start()
        both.wait_recv()
        rebuilt = total_out[...] + total_in[...] + dbias_ref[...].reshape(1, width)
        recon_ref[...] = jnp.where(core == 0, rebuilt[0:local_rows], rebuilt[local_rows:]).astype(BF16)
        block_two[...] = (rebuilt - acts[...]).astype(BF16)

        def during_last():
            loads[2].wait()
            loads[3].wait()

        arrive, finish_last = gather(
            block_two, residuals, (za_send, za_recv), (xa_send, xa_recv), (ca_send, ca_recv), during_last
        )

        def turn(far):
            residual_t[:, far * half_rows : (far + 1) * half_rows] = residuals[far].reshape(half_rows, width).T

        arrive(0)
        turn(0)
        slope[...] = jnp.dot(
            residual_t[:, :half_rows], active[:window].reshape(half_rows, feats), preferred_element_type=F32
        )
        arrive(1)
        turn(1)

        part = width // 4

        def store(i):
            where = pl.ds(i * part, part)
            return pltpu.make_async_copy(step.at[where], step_hbm.at[where], store_sem.at[i])

        for i in range(4):
            where = slice(i * part, (i + 1) * part)
            slope_rest = jnp.dot(
                residual_t[where, half_rows:], active[window:].reshape(half_rows, feats),
                preferred_element_type=F32,
            )
            gradient = 2.0 / total_rows * (slope[where] + slope_rest) + coef[...] * dec[where].astype(F32)
            moment_one = beta_one * first[where].astype(F32) + (1.0 - beta_one) * gradient
            moment_two = beta_two * second[where].astype(F32) + (1.0 - beta_two) * gradient * gradient
            step[where] = (
                moment_one * (1.0 / bias_one) / (jnp.sqrt(moment_two * (1.0 / bias_two)) + adam_eps)
            ).astype(BF16)
            store(i).start()

        finish_first()
        finish_last()
        each_far(lambda m: back_copy(m).wait_send())
        for copy in (*core_parts, both):
            copy.wait_send()
        for far, w in around:
            part_copy(far, w).wait_send()

        @pl.loop(1, peers)
        def _(j):
            square_copy(j).wait_send()
            sum_copy(j)[1].wait_send()
            active_copy(j).wait_send()

        for i in range(4):
            store(i).wait()

    scratch = [
        *(pltpu.VMEM((width, feats), BF16) for _ in range(5)),
        pltpu.SemaphoreType.DMA((4,)),
        pltpu.SemaphoreType.DMA((4,)),
        pltpu.VMEM((local_rows, width), BF16),
        pltpu.VMEM((local_rows, width), BF16),
        pltpu.VMEM((chip_rows, width), F32),
        pltpu.VMEM((2, window, per_chip, chip_rows, width), BF16),
        pltpu.VMEM((chip_rows, width), BF16),
        pltpu.VMEM((peers, group, feats), F32),
        pltpu.VMEM((peers, group, feats), BF16),
        pltpu.VMEM((peers, group, feats), BF16),
        pltpu.VMEM((peers, 2, core_rows, feats), BF16),
        pltpu.VMEM((8, feats), F32),
        pltpu.VMEM((peers, 8, feats), F32),
        pltpu.VMEM((2, 2, window, core_rows, width), F32),
        pltpu.VMEM((2, window, core_rows, width), F32),
        pltpu.VMEM((2, window, core_rows, width), BF16),
        pltpu.VMEM((2 * window, core_rows, width), BF16),
        pltpu.VMEM((per_core, chip_rows, width), BF16),
        pltpu.VMEM((per_core, chip_rows, width), BF16),
        pltpu.VMEM((chip_rows, width), F32),
        pltpu.VMEM((chip_rows, width), F32),
        pltpu.VMEM((2, window, per_chip, chip_rows, width), BF16),
        pltpu.VMEM((chip_rows, width), BF16),
        pltpu.VMEM((1, feats), F32),
        pltpu.VMEM((width, total_rows), BF16),
        pltpu.VMEM((width, feats), F32),
        *(pltpu.SemaphoreType.DMA((4,)) for _ in range(2)),
        *(pltpu.SemaphoreType.DMA((per_chip,)) for _ in range(6)),
        *(pltpu.SemaphoreType.DMA((2 * window,)) for _ in range(10)),
        *(pltpu.SemaphoreType.DMA((peers,)) for _ in range(6)),
    ]
    return kernel, scratch


def shards(nz, rows, reps, activations, enc_weight, enc_bias, dec_weight, dec_bias, first_moment, second_moment):
    local_rows, width = activations.shape
    feats = enc_weight.shape[1]
    kernel, scratch = make_kernel(nz, rows, reps, local_rows, width, feats)
    vmem = pl.BlockSpec(memory_space=pltpu.VMEM)
    hbm = pl.BlockSpec(memory_space=pl.ANY)
    recon, step = pl.pallas_call(
        kernel,
        out_shape=(
            jax.ShapeDtypeStruct((local_rows, width), BF16),
            jax.ShapeDtypeStruct((width, feats), BF16),
        ),
        in_specs=[vmem, hbm, vmem, hbm, vmem, hbm, hbm],
        out_specs=(vmem, hbm),
        scratch_shapes=scratch,
        compiler_params=pltpu.CompilerParams(
            collective_id=0, has_side_effects=True, vmem_limit_bytes=60 * 2**20
        ),
    )(activations, enc_weight, enc_bias, dec_weight.T, dec_bias, first_moment.T, second_moment.T)
    return recon, step.T


def solution(mesh):
    nz, rows, reps = mesh.shape["feat"] // 4, mesh.shape["row"], mesh.shape["rep"]

    def step(*args):
        return shards(nz, rows, reps, *args)

    return jax.shard_map(
        step,
        mesh=mesh,
        in_specs=(
            P("feat", ("row", "rep")),
            P(("row", "rep"), "feat"),
            P("feat"),
            P("feat", ("row", "rep")),
            P(("row", "rep")),
            P("feat", ("row", "rep")),
            P("feat", ("row", "rep")),
        ),
        out_specs=(P("feat", ("row", "rep")), P("feat", ("row", "rep"))),
        check_vma=False,
    )
```

time: 140 us -> 118 us (0.84)
  Pallas kernels: 133 us -> 114 us
  local copies, waits for them, and re-layouts: 5.88 us -> 3.19 us
    pallas_call x1, Pallas kernels: 133 us -> 114 us  [shards(): pl.pallas_call(kernel, out_shape=(jax.ShapeDtypeStruct((local_rows, width...]
    unnamed x14 -> x4, local copies, waits for them, and re-layouts: 4.13 us -> 3.19 us
where the time goes in v2:
time: 118 us
  Pallas kernels  114 us (97%)
  local copies, waits for them, and re-layouts  3.19 us (3%)
    pallas_call x1, Pallas kernels, shards(): pl.pallas_call(kernel, out_shape=(jax.ShapeDtypeStruct((local_rows, width...  114 us
    unnamed x4, local copies, waits for them, and re-layouts  3.19 us

profile of v2, /device:TPU:1, one launch (start us, length us, event | category | flops | bytes accessed | tf_op | source)
XLA Modules:
  0.0 118.1 jit_solution(10710393816067851580)
XLA Ops:
  0.6 114.3 %shard_map.86 = (bf16[4,576]{1,0:T(4,128)(2,1)}, bf16[576,512]{1,0:T(8,128)(2,1)}) custom-call(bf16[4,576]{1,0:T(4,128)(2,1)} %act_ref.1, bf16[576,512]{1,0:T(8,128)(2,1)} %enc_hbm.1, f32[512]{0:T(512)} %ebias_ref.1, bf16[576,512]{1,0:T(8,128)(2,1)} %bitcast.4, f32[576]{0:T(1024)} %dbias_ref.1, bf16[576,512]{1,0:T(8,128)(2,1)} %bitcast.5, ...), custom_call_target="tpu_custom_call" | custom-call | tf_op jit(solution)/shard_map/pallas_call | solution.py:421
  114.9 0.0 copy-start
  115.0 0.7 copy-done
  115.6 0.6 copy.11
  116.2 1.9 %copy.12 = bf16[512,576]{0,1:T(8,128)(2,1)} copy(bf16[512,576]{0,1:T(8,128)(2,1)} %bitcast.7) | data formatting | bytes 1179648
Async XLA Ops:
  114.9 0.7 copy-start

commit v3 on v2

--- a/solution.py
+++ b/solution.py
@@ -37,10 +37,10 @@
         recon_ref, step_hbm,
         enc, dec, first, second, step, load_sem, store_sem,
         act_send, act_recv, acts, gathered, block, partial, sums_out, sums_in, active,
-        squares_out, squares_in, product, core_in, parts_out, parts_in, z_out, z_in, total_out, total_in, residuals,
+        squares_out, squares_in, product, core_in, parts_out, parts_in, own_part, z_out, z_in, total_out, total_in, residuals,
         block_two, coef, residual_t, slope,
         pair_send, pair_recv, z_send, z_recv, zr_send, zr_recv, za_send, za_recv,
-        x_send, x_recv, c_send, c_recv, part_send, part_recv, xa_send, xa_recv, ca_send, ca_recv,
+        x_send, x_recv, xa_send, xa_recv, c_send, c_recv, ca_send, ca_recv, part_send, part_recv,
         peer_send, peer_recv, sq_send, sq_recv, ac_send, ac_recv,
     ):
         feat = lax.axis_index("feat")
@@ -137,6 +137,11 @@
                 def _():
                     action(m)
 
+        def each_mine(action):
+            @pl.loop(0, per_core)
+            def _(i):
+                action(core * per_core + i)
+
         mine = pl.ds(core * per_core, per_core)
 
         def gather(src, buffer, z_sems, x_sems, core_sems, between):
@@ -146,10 +151,11 @@
                     device_id=chip(0, z + window * (per_core - m)), device_id_type=MESH,
                 )
 
-            def beside_copy(far, w):
+            def beside_copy(far, w, m):
+                i = (far * window + w) * per_chip + m
                 return pltpu.make_async_remote_copy(
-                    src_ref=buffer.at[0, 0, mine], dst_ref=buffer.at[far, w, mine],
-                    send_sem=x_sems[0].at[far * window + w], recv_sem=x_sems[1].at[far * window + w],
+                    src_ref=buffer.at[0, 0, m], dst_ref=buffer.at[far, w, m],
+                    send_sem=x_sems[0].at[i], recv_sem=x_sems[1].at[i],
                     device_id=chip(far, z + near[w]), device_id_type=MESH,
                 )
 
@@ -167,15 +173,24 @@
                 buffer[0, 0, per_core] = src[...]
 
             between()
-            each_far(lambda m: z_copy(m).wait_recv())
-            for far, w in around:
-                beside_copy(far, w).start()
+
+            @pl.loop(0, per_core)
+            def _(i):
+                m, remote = far_first(per_core - 1 - i)
+
+                @pl.when(remote)
+                def _():
+                    z_copy(m).wait_recv()
+
+                for far, w in around:
+                    beside_copy(far, w, m).start()
+
             core_copy(0, 0).start()
 
             def arrive(far):
                 for w in range(window):
                     if (far, w) != (0, 0):
-                        beside_copy(far, w).wait_recv()
+                        each_mine(lambda m: beside_copy(far, w, m).wait_recv())
                         core_copy(far, w).start()
                 for w in range(window):
                     core_copy(far, w).wait_recv()
@@ -183,7 +198,7 @@
             def finish():
                 each_far(lambda m: z_copy(m).wait_send())
                 for far, w in around:
-                    beside_copy(far, w).wait_send()
+                    each_mine(lambda m: beside_copy(far, w, m).wait_send())
                     core_copy(far, w).wait_send()
                 core_copy(0, 0).wait_send()
 
@@ -200,54 +215,60 @@
             block, gathered, (z_send, z_recv), (x_send, x_recv), (c_send, c_recv), during_first
         )
 
-        def sum_copy(j):
+        def sum_copy(j, who):
             p = lax.rem(k + j, peers)
             return p, pltpu.make_async_remote_copy(
-                src_ref=sums_out.at[p], dst_ref=sums_in.at[j], send_sem=peer_send.at[j], recv_sem=peer_recv.at[j],
+                src_ref=sums_out.at[p, who], dst_ref=sums_in.at[j, who],
+                send_sem=peer_send.at[2 * j + who], recv_sem=peer_recv.at[2 * j + who],
                 device_id=peer(j), device_id_type=MESH,
             )
+
+        halves = (1 - core, core)
 
         def encode(far):
             rows_in = gathered[far].reshape(half_rows, width)
-            value = jnp.dot(rows_in, enc[...], preferred_element_type=F32).reshape(window, group, feats)
+            value = jnp.dot(rows_in, enc[...], preferred_element_type=F32).reshape(window, 2, core_rows, feats)
             partial[far * window : (far + 1) * window] = value
             sums_out[far * window : (far + 1) * window] = value.astype(BF16)
-
-            @pl.loop(1, peers)
-            def _(j):
-                p, copy = sum_copy(j)
-
-                @pl.when(lax.div(p, window) == far)
-                def _():
-                    copy.start()
+            for who in halves:
+
+                @pl.loop(1, peers)
+                def _(j):
+                    p, copy = sum_copy(j, who)
+
+                    @pl.when(lax.div(p, window) == far)
+                    def _():
+                        copy.start()
 
         arrive(0)
         encode(0)
         arrive(1)
         encode(1)
 
-        pre_sum = partial[k] + ebias_ref[...].reshape(1, feats)
-        for j in range(1, peers):
-            sum_copy(j)[1].wait_recv()
-            pre_sum += sums_in[j].astype(F32)
-        active[k] = jnp.maximum(pre_sum, 0.0).reshape(2, core_rows, feats).astype(BF16)
-
-        def active_copy(j):
+        def active_copy(j, who):
             return pltpu.make_async_remote_copy(
-                src_ref=active.at[k], dst_ref=active.at[k], send_sem=ac_send.at[j], recv_sem=ac_recv.at[j],
+                src_ref=active.at[k, who], dst_ref=active.at[k, who],
+                send_sem=ac_send.at[2 * j + who], recv_sem=ac_recv.at[2 * j + who],
                 device_id=peer(j), device_id_type=MESH,
             )
 
-        @pl.loop(1, peers)
-        def _(j):
-            active_copy(j).start()
-
-        def wait_active(far):
+        for who in halves:
+            pre_sum = partial[k, who] + ebias_ref[...].reshape(1, feats)
+            for j in range(1, peers):
+                sum_copy(j, who)[1].wait_recv()
+                pre_sum += sums_in[j, who].astype(F32)
+            active[k, who] = jnp.maximum(pre_sum, 0.0).astype(BF16)
+
+            @pl.loop(1, peers)
+            def _(j):
+                active_copy(j, who).start()
+
+        def wait_active(far, who):
             @pl.loop(1, peers)
             def _(j):
                 @pl.when(lax.div(lax.rem(k - j + peers, peers), window) == far)
                 def _():
-                    active_copy(j).wait_recv()
+                    active_copy(j, who).wait_recv()
 
         def decode(far, who):
             value = lax.dot_general(
@@ -258,36 +279,43 @@
 
         core_parts = [pair(product.at[far, 1 - core], core_in.at[far], 1 + far, other_core) for far in (0, 1)]
 
-        def part_copy(far, w):
+        def part_copy(far, w, place):
+            i = (far * window + w) * per_core + place
             return pltpu.make_async_remote_copy(
-                src_ref=parts_out.at[far, w], dst_ref=parts_in.at[far * window + w],
-                send_sem=part_send.at[far * window + w], recv_sem=part_recv.at[far * window + w],
+                src_ref=parts_out.at[far, w, place], dst_ref=parts_in.at[far * window + w, place],
+                send_sem=part_send.at[i], recv_sem=part_recv.at[i],
                 device_id=chip(far, z - near[w]), device_id_type=MESH,
             )
+
+        def place_of(j):
+            return jnp.where(core == 0, j, per_core - 1 - j)
 
         def hand_out(far):
             core_parts[far].wait_recv()
             both_cores = product[far, core] + core_in[far]
+            both_cores = both_cores.reshape(window, per_core, chip_rows, width)
             parts_out[far] = both_cores.astype(BF16)
-            for other, w in around:
-                if other == far:
-                    part_copy(far, w).start()
+
+            @pl.loop(0, per_core)
+            def _(j):
+                for other, w in around:
+                    if other == far:
+                        part_copy(far, w, place_of(j)).start()
+
             return both_cores
 
-        wait_active(0)
+        wait_active(0, 1 - core)
         decode(0, 1 - core)
         core_parts[0].start()
-        decode(0, core)
-        wait_active(1)
+        wait_active(1, 1 - core)
         decode(1, 1 - core)
         core_parts[1].start()
-        own_part = hand_out(0)[0]
+        wait_active(0, core)
+        decode(0, core)
+        own_part[...] = hand_out(0)[0]
+        wait_active(1, core)
         decode(1, core)
         hand_out(1)
-        for far, w in reversed(around):
-            part_copy(far, w).wait_recv()
-            own_part += parts_in[far * window + w].astype(F32)
-        z_out[...] = own_part.reshape(per_core, chip_rows, width).astype(BF16)
 
         def back_copy(m):
             place = m - core * per_core
@@ -296,7 +324,19 @@
                 device_id=chip(0, z + window * (m - per_core)), device_id_type=MESH,
             )
 
-        each_far(lambda m: back_copy(m).start())
+        @pl.loop(0, per_core)
+        def _(j):
+            place = place_of(j)
+            value = own_part[place]
+            for far, w in reversed(around):
+                part_copy(far, w, place).wait_recv()
+                value += parts_in[far * window + w, place].astype(F32)
+            z_out[place] = value.astype(BF16)
+            m, remote = far_first(j)
+
+            @pl.when(remote)
+            def _():
+                back_copy(m).start()
 
         @pl.when(core == 1)
         def _():
@@ -364,14 +404,18 @@
         each_far(lambda m: back_copy(m).wait_send())
         for copy in (*core_parts, both):
             copy.wait_send()
-        for far, w in around:
-            part_copy(far, w).wait_send()
+
+        @pl.loop(0, per_core)
+        def _(j):
+            for far, w in around:
+                part_copy(far, w, j).wait_send()
 
         @pl.loop(1, peers)
         def _(j):
             square_copy(j).wait_send()
-            sum_copy(j)[1].wait_send()
-            active_copy(j).wait_send()
+            for who in (0, 1):
+                sum_copy(j, who)[1].wait_send()
+                active_copy(j, who).wait_send()
 
         for i in range(4):
             store(i).wait()
@@ -385,16 +429,15 @@
         pltpu.VMEM((chip_rows, width), F32),
         pltpu.VMEM((2, window, per_chip, chip_rows, width), BF16),
         pltpu.VMEM((chip_rows, width), BF16),
-        pltpu.VMEM((peers, group, feats), F32),
-        pltpu.VMEM((peers, group, feats), BF16),
-        pltpu.VMEM((peers, group, feats), BF16),
-        pltpu.VMEM((peers, 2, core_rows, feats), BF16),
+        pltpu.VMEM((peers, 2, core_rows, feats), F32),
+        *(pltpu.VMEM((peers, 2, core_rows, feats), BF16) for _ in range(3)),
         pltpu.VMEM((8, feats), F32),
         pltpu.VMEM((peers, 8, feats), F32),
         pltpu.VMEM((2, 2, window, core_rows, width), F32),
         pltpu.VMEM((2, window, core_rows, width), F32),
-        pltpu.VMEM((2, window, core_rows, width), BF16),
-        pltpu.VMEM((2 * window, core_rows, width), BF16),
+        pltpu.VMEM((2, window, per_core, chip_rows, width), BF16),
+        pltpu.VMEM((2 * window, per_core, chip_rows, width), BF16),
+        pltpu.VMEM((per_core, chip_rows, width), F32),
         pltpu.VMEM((per_core, chip_rows, width), BF16),
         pltpu.VMEM((per_core, chip_rows, width), BF16),
         pltpu.VMEM((chip_rows, width), F32),
@@ -406,8 +449,12 @@
         pltpu.VMEM((width, feats), F32),
         *(pltpu.SemaphoreType.DMA((4,)) for _ in range(2)),
         *(pltpu.SemaphoreType.DMA((per_chip,)) for _ in range(6)),
-        *(pltpu.SemaphoreType.DMA((2 * window,)) for _ in range(10)),
-        *(pltpu.SemaphoreType.DMA((peers,)) for _ in range(6)),
+        *(pltpu.SemaphoreType.DMA((2 * window * per_chip,)) for _ in range(4)),
+        *(pltpu.SemaphoreType.DMA((2 * window,)) for _ in range(4)),
+        *(pltpu.SemaphoreType.DMA((2 * window * per_core,)) for _ in range(2)),
+        *(pltpu.SemaphoreType.DMA((2 * peers,)) for _ in range(2)),
+        *(pltpu.SemaphoreType.DMA((peers,)) for _ in range(2)),
+        *(pltpu.SemaphoreType.DMA((2 * peers,)) for _ in range(2)),
     ]
     return kernel, scratch
 
@@ -428,7 +475,7 @@
         out_specs=(vmem, hbm),
         scratch_shapes=scratch,
         compiler_params=pltpu.CompilerParams(
-            collective_id=0, has_side_effects=True, vmem_limit_bytes=60 * 2**20
+            collective_id=0, has_side_effects=True, vmem_limit_bytes=53 * 2**20
         ),
     )(activations, enc_weight, enc_bias, dec_weight.T, dec_bias, first_moment.T, second_moment.T)
     return recon, step.T

time: 118 us -> 114 us (0.966)
  Pallas kernels: 114 us -> 110 us
    pallas_call x1, Pallas kernels: 114 us -> 110 us  [shards(): pl.pallas_call(kernel, out_shape=(jax.ShapeDtypeStruct((local_rows, width...]
    unnamed x4 -> x8, local copies, waits for them, and re-layouts: 3.19 us -> 3.46 us
where the time goes in v3:
time: 114 us
  Pallas kernels  110 us (96%)
  local copies, waits for them, and re-layouts  3.46 us (3%)
    pallas_call x1, Pallas kernels, shards(): pl.pallas_call(kernel, out_shape=(jax.ShapeDtypeStruct((local_rows, width...  110 us
    unnamed x8, local copies, waits for them, and re-layouts  3.46 us

profile of v3, /device:TPU:1, one launch (start us, length us, event | category | flops | bytes accessed | tf_op | source)
XLA Modules:
  0.0 113.9 jit_solution(5740209833754268368)
XLA Ops:
  0.6 0.0 copy-start
  0.6 0.7 copy-done
  1.3 0.0 copy-start.1
  1.3 0.7 copy-done.1
  2.0 0.0 copy-start.2
  2.0 0.7 copy-done.2
  2.7 109.8 %shard_map.86 = (bf16[4,576]{1,0:T(4,128)(2,1)S(1)}, bf16[576,512]{1,0:T(8,128)(2,1)S(1)}) custom-call(bf16[4,576]{1,0:T(4,128)(2,1)S(1)} %copy-done, bf16[576,512]{1,0:T(8,128)(2,1)} %enc_hbm.1, f32[512]{0:T(512)S(1)} %copy-done.2, bf16[576,512]{1,0:T(8,128)(2,1)} %bitcast.5, f32[576]{0:T(1024)S(1)} %copy-done.1, bf16[576,512]{1,0:T(8,128)(2,1)} %bitcast.6, ...), custom_call_target="tpu_custom_call" | custom-call | tf_op jit(solution)/shard_map/pallas_call | solution.py:468
  112.5 0.6 copy.11
  113.1 0.8 copy.12
Async XLA Ops:
  0.6 0.7 copy-start
  1.3 0.7 copy-start.1
  2.0 0.7 copy-start.2

commit v4 on v3

--- a/solution.py
+++ b/solution.py
@@ -75,17 +75,15 @@
             pl.semaphore_signal(barrier, inc=1, device_id=device, device_id_type=MESH)
 
         def far_first(j):
-            m = jnp.where(core == 0, j, per_chip - 1 - j)
-            return m, m != per_core
+            return jnp.where(core == 0, j, per_chip - 1 - j)
+
+        def away(m):
+            return window * (m - per_core) + window // 2
 
         @pl.loop(0, per_core)
         def _(j):
-            m, remote = far_first(j)
-
-            @pl.when(remote)
-            def _():
-                greet(chip(0, z + window * (per_core - m)))
-                greet(chip(0, z - window * (per_core - m)))
+            greet(chip(0, z + away(far_first(j))))
+            greet(chip(0, z - away(far_first(j))))
 
         beside = sorted({(far, side * near[w]) for far, w in around for side in (1, -1)})
         for far, offset in beside:
@@ -106,7 +104,7 @@
         squares_out[...] = jnp.dot(ones, high, preferred_element_type=F32) + jnp.dot(
             ones, rest, preferred_element_type=F32
         )
-        pl.semaphore_wait(barrier, 2 * per_core - 2 * core + len(beside) + peers)
+        pl.semaphore_wait(barrier, 2 * per_core + len(beside) + peers)
 
         def pair(src, dst, i, device):
             return pltpu.make_async_remote_copy(
@@ -131,11 +129,7 @@
         def each_far(action):
             @pl.loop(0, per_core)
             def _(j):
-                m, remote = far_first(j)
-
-                @pl.when(remote)
-                def _():
-                    action(m)
+                action(far_first(j))
 
         def each_mine(action):
             @pl.loop(0, per_core)
@@ -148,7 +142,7 @@
             def z_copy(m):
                 return pltpu.make_async_remote_copy(
                     src_ref=src, dst_ref=buffer.at[0, 0, m], send_sem=z_sems[0].at[m], recv_sem=z_sems[1].at[m],
-                    device_id=chip(0, z + window * (per_core - m)), device_id_type=MESH,
+                    device_id=chip(0, z - away(m)), device_id_type=MESH,
                 )
 
             def beside_copy(far, w, m):
@@ -168,20 +162,12 @@
 
             each_far(lambda m: z_copy(m).start())
 
-            @pl.when(core == 1)
-            def _():
-                buffer[0, 0, per_core] = src[...]
-
             between()
 
             @pl.loop(0, per_core)
             def _(i):
-                m, remote = far_first(per_core - 1 - i)
-
-                @pl.when(remote)
-                def _():
-                    z_copy(m).wait_recv()
-
+                m = far_first(per_core - 1 - i)
+                z_copy(m).wait_recv()
                 for far, w in around:
                     beside_copy(far, w, m).start()
 
@@ -195,14 +181,16 @@
                 for w in range(window):
                     core_copy(far, w).wait_recv()
 
-            def finish():
+            def finish_beside():
                 each_far(lambda m: z_copy(m).wait_send())
                 for far, w in around:
                     each_mine(lambda m: beside_copy(far, w, m).wait_send())
-                    core_copy(far, w).wait_send()
-                core_copy(0, 0).wait_send()
-
-            return arrive, finish
+
+            def finish_core():
+                for i in range(2 * window):
+                    core_copy(i // window, i % window).wait_send()
+
+            return arrive, finish_beside, finish_core
 
         def during_first():
             @pl.loop(1, peers)
@@ -211,7 +199,7 @@
 
             loads[1].wait()
 
-        arrive, finish_first = gather(
+        arrive, finish_beside, finish_core = gather(
             block, gathered, (z_send, z_recv), (x_send, x_recv), (c_send, c_recv), during_first
         )
 
@@ -321,7 +309,7 @@
             place = m - core * per_core
             return pltpu.make_async_remote_copy(
                 src_ref=z_out.at[place], dst_ref=z_in.at[place], send_sem=zr_send.at[m], recv_sem=zr_recv.at[m],
-                device_id=chip(0, z + window * (m - per_core)), device_id_type=MESH,
+                device_id=chip(0, z + away(m)), device_id_type=MESH,
             )
 
         @pl.loop(0, per_core)
@@ -332,15 +320,7 @@
                 part_copy(far, w, place).wait_recv()
                 value += parts_in[far * window + w, place].astype(F32)
             z_out[place] = value.astype(BF16)
-            m, remote = far_first(j)
-
-            @pl.when(remote)
-            def _():
-                back_copy(m).start()
-
-        @pl.when(core == 1)
-        def _():
-            z_in[0] = z_out[0]
+            back_copy(far_first(j)).start()
 
         flat = active[...].reshape(total_rows, feats)
         counts = jnp.dot(jnp.ones((8, total_rows), BF16), flat, preferred_element_type=F32)
@@ -363,8 +343,26 @@
         def during_last():
             loads[2].wait()
             loads[3].wait()
-
-        arrive, finish_last = gather(
+            finish_beside()
+            finish_core()
+            each_far(lambda m: back_copy(m).wait_send())
+            for copy in (*core_parts, both):
+                copy.wait_send()
+
+            @pl.loop(0, per_core)
+            def _(j):
+                for far, w in around:
+                    part_copy(far, w, j).wait_send()
+
+            @pl.loop(1, peers)
+            def _(j):
+                square_copy(j).wait_send()
+                for who in (0, 1):
+                    sum_copy(j, who)[1].wait_send()
+                    active_copy(j, who).wait_send()
+
+
+        arrive, finish_beside_last, finish_core_last = gather(
             block_two, residuals, (za_send, za_recv), (xa_send, xa_recv), (ca_send, ca_recv), during_last
         )
 
@@ -373,9 +371,10 @@
 
         arrive(0)
         turn(0)
-        slope[...] = jnp.dot(
+        slope[...] = 2.0 / total_rows * jnp.dot(
             residual_t[:, :half_rows], active[:window].reshape(half_rows, feats), preferred_element_type=F32
-        )
+        ) + coef[...] * dec[...].astype(F32)
+        finish_beside_last()
         arrive(1)
         turn(1)
 
@@ -391,7 +390,7 @@
                 residual_t[where, half_rows:], active[window:].reshape(half_rows, feats),
                 preferred_element_type=F32,
             )
-            gradient = 2.0 / total_rows * (slope[where] + slope_rest) + coef[...] * dec[where].astype(F32)
+            gradient = slope[where] + 2.0 / total_rows * slope_rest
             moment_one = beta_one * first[where].astype(F32) + (1.0 - beta_one) * gradient
             moment_two = beta_two * second[where].astype(F32) + (1.0 - beta_two) * gradient * gradient
             step[where] = (
@@ -399,24 +398,7 @@
             ).astype(BF16)
             store(i).start()
 
-        finish_first()
-        finish_last()
-        each_far(lambda m: back_copy(m).wait_send())
-        for copy in (*core_parts, both):
-            copy.wait_send()
-
-        @pl.loop(0, per_core)
-        def _(j):
-            for far, w in around:
-                part_copy(far, w, j).wait_send()
-
-        @pl.loop(1, peers)
-        def _(j):
-            square_copy(j).wait_send()
-            for who in (0, 1):
-                sum_copy(j, who)[1].wait_send()
-                active_copy(j, who).wait_send()
-
+        finish_core_last()
         for i in range(4):
             store(i).wait()
 
@@ -475,7 +457,7 @@
         out_specs=(vmem, hbm),
         scratch_shapes=scratch,
         compiler_params=pltpu.CompilerParams(
-            collective_id=0, has_side_effects=True, vmem_limit_bytes=53 * 2**20
+            collective_id=0, has_side_effects=True, vmem_limit_bytes=60 * 2**20
         ),
     )(activations, enc_weight, enc_bias, dec_weight.T, dec_bias, first_moment.T, second_moment.T)
     return recon, step.T

time: 114 us -> 110 us (0.965)
  Pallas kernels: 110 us -> 106 us
    pallas_call x1, Pallas kernels: 110 us -> 106 us  [shards(): pl.pallas_call(kernel, out_shape=(jax.ShapeDtypeStruct((local_rows, width...]
    unnamed x8 -> x4, local copies, waits for them, and re-layouts: 3.46 us -> 3.19 us
where the time goes in v4:
time: 110 us; the launch traced here: 109 us
  Pallas kernels  106 us (96%)
  local copies, waits for them, and re-layouts  3.19 us (3%)
    pallas_call x1, Pallas kernels, shards(): pl.pallas_call(kernel, out_shape=(jax.ShapeDtypeStruct((local_rows, width...  106 us
    unnamed x4, local copies, waits for them, and re-layouts  3.19 us

profile of v4, /device:TPU:1, one launch (start us, length us, event | category | flops | bytes accessed | tf_op | source)
XLA Modules:
  0.0 109.4 jit_solution(16527439030619427099)
XLA Ops:
  0.6 105.6 %shard_map.86 = (bf16[4,576]{1,0:T(4,128)(2,1)}, bf16[576,512]{1,0:T(8,128)(2,1)}) custom-call(bf16[4,576]{1,0:T(4,128)(2,1)} %act_ref.1, bf16[576,512]{1,0:T(8,128)(2,1)} %enc_hbm.1, f32[512]{0:T(512)} %ebias_ref.1, bf16[576,512]{1,0:T(8,128)(2,1)} %bitcast.4, f32[576]{0:T(1024)} %dbias_ref.1, bf16[576,512]{1,0:T(8,128)(2,1)} %bitcast.5, ...), custom_call_target="tpu_custom_call" | custom-call | tf_op jit(solution)/shard_map/pallas_call | solution.py:450
  106.2 0.0 copy-start
  106.3 0.7 copy-done
  106.9 0.6 copy.11
  107.5 1.9 %copy.12 = bf16[512,576]{0,1:T(8,128)(2,1)} copy(bf16[512,576]{0,1:T(8,128)(2,1)} %bitcast.7) | data formatting | bytes 1179648
Async XLA Ops:
  106.2 0.7 copy-start

commit v5 on v4

--- a/solution.py
+++ b/solution.py
@@ -33,9 +33,9 @@
     around = [(far, w) for far in (1, 0) for w in range(window) if (far, w) != (0, 0)]
 
     def kernel(
-        act_ref, enc_hbm, ebias_ref, dec_hbm, dbias_ref, first_hbm, second_hbm,
-        recon_ref, step_hbm,
-        enc, dec, first, second, step, load_sem, store_sem,
+        act_hbm, enc_hbm, ebias_hbm, dec_hbm, dbias_hbm, first_hbm, second_hbm,
+        recon_hbm, step_hbm,
+        ebias_ref, dbias_ref, recon_ref, enc, dec, first, second, step, load_sem, store_sem,
         act_send, act_recv, acts, gathered, block, partial, sums_out, sums_in, active,
         squares_out, squares_in, product, core_in, parts_out, parts_in, own_part, z_out, z_in, total_out, total_in, residuals,
         block_two, coef, residual_t, slope,
@@ -63,7 +63,10 @@
         loads = [
             pltpu.make_async_copy(src, dst, load_sem.at[i])
             for i, (src, dst) in enumerate(
-                ((dec_hbm, dec), (enc_hbm, enc), (first_hbm, first), (second_hbm, second))
+                (
+                    (act_hbm, act_send), (dbias_hbm, dbias_ref), (dec_hbm, dec), (enc_hbm, enc),
+                    (ebias_hbm, ebias_ref), (first_hbm, first), (second_hbm, second),
+                )
             )
         ]
         for load in loads:
@@ -94,8 +97,8 @@
         def _(j):
             greet(peer(j))
 
-        act_send[...] = act_ref[...]
-        loads[0].wait()
+        for load in loads[:3]:
+            load.wait()
         wide = dec[...].astype(F32)
         square = wide * wide
         high = square.astype(BF16)
@@ -197,7 +200,8 @@
             def _(j):
                 square_copy(j).start()
 
-            loads[1].wait()
+            loads[3].wait()
+            loads[4].wait()
 
         arrive, finish_beside, finish_core = gather(
             block, gathered, (z_send, z_recv), (x_send, x_recv), (c_send, c_recv), during_first
@@ -338,11 +342,14 @@
         both.wait_recv()
         rebuilt = total_out[...] + total_in[...] + dbias_ref[...].reshape(1, width)
         recon_ref[...] = jnp.where(core == 0, rebuilt[0:local_rows], rebuilt[local_rows:]).astype(BF16)
+        store_recon = pltpu.make_async_copy(recon_ref, recon_hbm, store_sem.at[4])
+        store_recon.start()
         block_two[...] = (rebuilt - acts[...]).astype(BF16)
 
         def during_last():
-            loads[2].wait()
-            loads[3].wait()
+            loads[5].wait()
+            loads[6].wait()
+            store_recon.wait()
             finish_beside()
             finish_core()
             each_far(lambda m: back_copy(m).wait_send())
@@ -403,9 +410,12 @@
             store(i).wait()
 
     scratch = [
+        pltpu.VMEM((feats,), F32),
+        pltpu.VMEM((width,), F32),
+        pltpu.VMEM((local_rows, width), BF16),
         *(pltpu.VMEM((width, feats), BF16) for _ in range(5)),
-        pltpu.SemaphoreType.DMA((4,)),
-        pltpu.SemaphoreType.DMA((4,)),
+        pltpu.SemaphoreType.DMA((7,)),
+        pltpu.SemaphoreType.DMA((5,)),
         pltpu.VMEM((local_rows, width), BF16),
         pltpu.VMEM((local_rows, width), BF16),
         pltpu.VMEM((chip_rows, width), F32),
@@ -441,11 +451,48 @@
     return kernel, scratch
 
 
+def hand_over(recon, step):
+    parts = 4
+    part = step.shape[0] // parts
+
+    def kernel(recon_in, step_in, recon_out, step_out, recon_held, step_held, in_sems, out_sems):
+        where = [pl.ds(i * part, part) for i in range(parts)]
+        arrive = [pltpu.make_async_copy(recon_in, recon_held, in_sems.at[parts])]
+        leave = [pltpu.make_async_copy(recon_held, recon_out, out_sems.at[parts])]
+        for i, rows in enumerate(where):
+            arrive.append(pltpu.make_async_copy(step_in.at[rows], step_held.at[rows], in_sems.at[i]))
+            leave.append(pltpu.make_async_copy(step_held.at[rows], step_out.at[rows], out_sems.at[i]))
+        for copy in arrive:
+            copy.start()
+        for one, two in zip(arrive, leave):
+            one.wait()
+            two.start()
+        for copy in leave:
+            copy.wait()
+
+    hbm = pl.BlockSpec(memory_space=pl.ANY)
+    return pl.pallas_call(
+        kernel,
+        out_shape=(
+            jax.ShapeDtypeStruct(recon.shape, recon.dtype),
+            jax.ShapeDtypeStruct(step.shape, step.dtype),
+        ),
+        in_specs=[hbm, hbm],
+        out_specs=(hbm, hbm),
+        scratch_shapes=[
+            pltpu.VMEM(recon.shape, recon.dtype),
+            pltpu.VMEM(step.shape, step.dtype),
+            pltpu.SemaphoreType.DMA((parts + 1,)),
+            pltpu.SemaphoreType.DMA((parts + 1,)),
+        ],
+        compiler_params=pltpu.CompilerParams(vmem_limit_bytes=60 * 2**20),
+    )(recon, step)
+
+
 def shards(nz, rows, reps, activations, enc_weight, enc_bias, dec_weight, dec_bias, first_moment, second_moment):
     local_rows, width = activations.shape
     feats = enc_weight.shape[1]
     kernel, scratch = make_kernel(nz, rows, reps, local_rows, width, feats)
-    vmem = pl.BlockSpec(memory_space=pltpu.VMEM)
     hbm = pl.BlockSpec(memory_space=pl.ANY)
     recon, step = pl.pallas_call(
         kernel,
@@ -453,13 +500,14 @@
             jax.ShapeDtypeStruct((local_rows, width), BF16),
             jax.ShapeDtypeStruct((width, feats), BF16),
         ),
-        in_specs=[vmem, hbm, vmem, hbm, vmem, hbm, hbm],
-        out_specs=(vmem, hbm),
+        in_specs=[hbm] * 7,
+        out_specs=(hbm, hbm),
         scratch_shapes=scratch,
         compiler_params=pltpu.CompilerParams(
             collective_id=0, has_side_effects=True, vmem_limit_bytes=60 * 2**20
         ),
     )(activations, enc_weight, enc_bias, dec_weight.T, dec_bias, first_moment.T, second_moment.T)
+    recon, step = hand_over(recon, step)
     return recon, step.T
 
 

time: 110 us -> 107 us (0.973)
  local copies, waits for them, and re-layouts: 3.19 us -> 0 us
    unnamed x4 -> x0, local copies, waits for them, and re-layouts: 3.19 us -> none
    pallas_call x0 -> x1, Pallas kernels: none -> 1.89 us  [hand_over(): pl.pallas_call(kernel, out_shape=(jax.ShapeDtypeStruct(recon.shape, recon...]
where the time goes in v5:
time: 107 us
  Pallas kernels  107 us (100%)
    pallas_call x1, Pallas kernels, shards(): pl.pallas_call(kernel, out_shape=(jax.ShapeDtypeStruct((local_rows, width...  105 us

profile of v5, /device:TPU:1, one launch (start us, length us, event | category | flops | bytes accessed | tf_op | source)
XLA Modules:
  0.0 107.3 jit_solution(8215566343350683146)
XLA Ops:
  0.6 104.7 %shard_map.86 = (bf16[4,576]{1,0:T(4,128)(2,1)}, bf16[576,512]{1,0:T(8,128)(2,1)}) custom-call(bf16[4,576]{1,0:T(4,128)(2,1)} %act_hbm.1, bf16[576,512]{1,0:T(8,128)(2,1)} %enc_hbm.1, f32[512]{0:T(512)} %ebias_hbm.1, bf16[576,512]{1,0:T(8,128)(2,1)} %bitcast.4, f32[576]{0:T(1024)} %dbias_hbm.1, bf16[576,512]{1,0:T(8,128)(2,1)} %bitcast.5, ...), custom_call_target="tpu_custom_call" | custom-call | tf_op jit(solution)/shard_map/pallas_call | solution.py:497
  105.4 1.9 %shard_map.87 = (bf16[4,576]{1,0:T(4,128)(2,1)}, bf16[576,512]{1,0:T(8,128)(2,1)}) custom-call(bf16[4,576]{1,0:T(4,128)(2,1)} %get-tuple-element.6.recon_in, bf16[576,512]{1,0:T(8,128)(2,1)} %get-tuple-element.7.step_in), custom_call_target="tpu_custom_call" | custom-call | tf_op jit(solution)/shard_map/pallas_call | solution.py:474

commit v6 on v5

--- a/solution.py
+++ b/solution.py
@@ -69,9 +69,6 @@
                 )
             )
         ]
-        for load in loads:
-            load.start()
-
         barrier = pltpu.get_barrier_semaphore()
 
         def greet(device):
@@ -97,6 +94,8 @@
         def _(j):
             greet(peer(j))
 
+        for load in loads:
+            load.start()
         for load in loads[:3]:
             load.wait()
         wide = dec[...].astype(F32)

time: 107 us -> 107 us (level)
  no operation moved by 1% of the time
where the time goes in v6:
time: 107 us
  Pallas kernels  106 us (99%)
    pallas_call x1, Pallas kernels, shards(): pl.pallas_call(kernel, out_shape=(jax.ShapeDtypeStruct((local_rows, width...  104 us

profile of v6, /device:TPU:1, one launch (start us, length us, event | category | flops | bytes accessed | tf_op | source)
XLA Modules:
  0.0 106.9 jit_solution(3486705154188304039)
XLA Ops:
  0.6 104.4 %shard_map.86 = (bf16[4,576]{1,0:T(4,128)(2,1)}, bf16[576,512]{1,0:T(8,128)(2,1)}) custom-call(bf16[4,576]{1,0:T(4,128)(2,1)} %act_hbm.1, bf16[576,512]{1,0:T(8,128)(2,1)} %enc_hbm.1, f32[512]{0:T(512)} %ebias_hbm.1, bf16[576,512]{1,0:T(8,128)(2,1)} %bitcast.4, f32[576]{0:T(1024)} %dbias_hbm.1, bf16[576,512]{1,0:T(8,128)(2,1)} %bitcast.5, ...), custom_call_target="tpu_custom_call" | custom-call | tf_op jit(solution)/shard_map/pallas_call | solution.py:496
  105.0 1.9 %shard_map.87 = (bf16[4,576]{1,0:T(4,128)(2,1)}, bf16[576,512]{1,0:T(8,128)(2,1)}) custom-call(bf16[4,576]{1,0:T(4,128)(2,1)} %get-tuple-element.6.recon_in, bf16[576,512]{1,0:T(8,128)(2,1)} %get-tuple-element.7.step_in), custom_call_target="tpu_custom_call" | custom-call | tf_op jit(solution)/shard_map/pallas_call | solution.py:473
